TPU v7x, 32 devices: a whole 2x2x4 slice. The times are simulated.
32 devices in a mesh: dp: 4 (over z), expert: 8 (over y, x, core).
Axes of the slice: x: 2, y: 2, z: 4, core: 2. Of those that a mesh axis runs over, the one named last changes fastest.
Arguments:
- tokens: bfloat16 [4096, 4096], P(('dp', 'expert')), may hold values from -6 to 6
- expert_ids: int32 [4096, 2], P(('dp', 'expert')), may hold values from 0 to 7, all different within a row; in each aligned block of 128 rows (0 to 127, 128 to 255, ...) at most 36 rows name the same one
- router_probs: float32 [4096, 2], P(('dp', 'expert')), may hold values from 0.1 to 1
- w_gate: bfloat16 [8, 1024, 4096], P('expert', 'dp'), may hold values from -0.09375 to 0.09375
- w_up: bfloat16 [8, 1024, 4096], P('expert', 'dp'), may hold values from -0.09375 to 0.09375
- w_down: bfloat16 [8, 1024, 4096], P('expert', 'dp'), may hold values from -0.1875 to 0.1875
- out_grad: bfloat16 [4096, 4096], P(('dp', 'expert')), may hold values from -6 to 6
Outputs:
- mixed: bfloat16 [4096, 4096], P(('dp', 'expert'))
- input_grad: bfloat16 [4096, 4096], P(('dp', 'expert'))
- prob_grad: float32 [4096, 2], P(('dp', 'expert'))
- grad_gate: bfloat16 [8, 1024, 4096], P('expert', 'dp')
- grad_up: bfloat16 [8, 1024, 4096], P('expert', 'dp')
- grad_down: bfloat16 [8, 1024, 4096], P('expert', 'dp')
Inputs may be any that keep to these rules, and one draw needn't show every extreme that they name: `expert_ids`: each row names 2 different experts. Among the rows of one device no expert is named more than 36 times, a bound that some block reaches.
All inputs are finite; a program needn't handle non-finite values.
Results may differ from a plain program's by a relative error of at most 0.018.
Values may be sent and summed in bfloat16 or wider, within the bound.
A program may use at most 192 MiB of HBM per device.

v0:
```python
import jax
import jax.numpy as jnp
from jax import lax
from jax.sharding import PartitionSpec as P


def deliver(stacked):
    moved_rows = lax.all_to_all(stacked, "expert", split_axis=1, concat_axis=1, tiled=True)
    arrived = lax.all_gather(moved_rows[None], "dp", axis=0, tiled=True)
    return arrived


def send_back(stacked):
    return lax.all_to_all(stacked, "expert", split_axis=1, concat_axis=1, tiled=True)


def on_device(tokens, expert_ids, router_probs, w_gate, w_up, w_down, out_grad):
    tok_rows, model_width = tokens.shape
    top_count = expert_ids.shape[1]
    local_experts = w_gate.shape[0]
    n_expert = lax.axis_size("expert")
    n_replica = lax.axis_size("dp")
    experts = local_experts * n_expert
    slot_depth = max(2, tok_rows * top_count * 9 // (8 * experts))
    slot_total = experts * slot_depth
    blocks = n_replica * n_expert
    flat_ids = expert_ids.reshape(-1)
    onehot = (flat_ids[:, None] == jnp.arange(experts, dtype=jnp.int32)[None, :]).astype(jnp.int32)
    earlier = jnp.cumsum(onehot, axis=0) - onehot
    rank_of = jnp.sum(earlier * onehot, axis=1)
    slot_of = flat_ids * slot_depth + rank_of
    selector = (jnp.arange(slot_total, dtype=jnp.int32)[:, None] == slot_of[None, :]).astype(
        jnp.bfloat16
    )
    by_token = jnp.sum(selector.reshape(slot_total, tok_rows, top_count), axis=2)
    send_tokens = jnp.dot(by_token, tokens, preferred_element_type=jnp.float32).astype(jnp.bfloat16)
    send_tokens = send_tokens.reshape(n_expert, local_experts, slot_depth, model_width)
    scaled = (
        router_probs.reshape(-1)[:, None]
        * jnp.repeat(out_grad, top_count, axis=0).astype(jnp.float32)
    ).astype(jnp.bfloat16)
    send_grads = jnp.dot(selector, scaled, preferred_element_type=jnp.float32).astype(jnp.bfloat16)
    send_grads = send_grads.reshape(n_expert, local_experts, slot_depth, model_width)
    block_shape = (blocks, local_experts, slot_depth, model_width)
    rows_in = deliver(send_tokens[None])[:, 0].reshape(block_shape)
    gate_proj = jnp.einsum("sxmd,xfd->sxmf", rows_in, w_gate, preferred_element_type=jnp.float32)
    up_proj = jnp.einsum("sxmd,xfd->sxmf", rows_in, w_up, preferred_element_type=jnp.float32)
    sigmoid_gate = jax.nn.sigmoid(gate_proj)
    activated = gate_proj * sigmoid_gate
    hidden = (activated * up_proj).astype(jnp.bfloat16)
    expert_out = lax.psum_scatter(
        jnp.einsum("sxmf,xfd->sxmd", hidden, w_down, preferred_element_type=jnp.float32).astype(
            jnp.bfloat16
        ),
        "dp",
        scatter_dimension=0,
        tiled=True,
    )
    back_out = send_back(expert_out[None])[0]
    grads_in = deliver(send_grads[None])[:, 0].reshape(block_shape)
    d_hidden = jnp.einsum("sxmd,xfd->sxmf", grads_in, w_down, preferred_element_type=jnp.float32)
    grad_down = jnp.einsum(
        "sxmf,sxmd->xfd", hidden, grads_in, preferred_element_type=jnp.float32
    ).astype(jnp.bfloat16)
    d_gate = (d_hidden * up_proj * sigmoid_gate * (1.0 + gate_proj * (1.0 - sigmoid_gate))).astype(
        jnp.bfloat16
    )
    d_up = (d_hidden * activated).astype(jnp.bfloat16)
    grad_gate = jnp.einsum(
        "sxmf,sxmd->xfd", d_gate, rows_in, preferred_element_type=jnp.float32
    ).astype(jnp.bfloat16)
    grad_up = jnp.einsum(
        "sxmf,sxmd->xfd", d_up, rows_in, preferred_element_type=jnp.float32
    ).astype(jnp.bfloat16)
    total = jnp.einsum("sxmf,xfd->sxmd", d_gate, w_gate, preferred_element_type=jnp.float32)
    expert_dx = lax.psum_scatter(
        (
            total + jnp.einsum("sxmf,xfd->sxmd", d_up, w_up, preferred_element_type=jnp.float32)
        ).astype(jnp.bfloat16),
        "dp",
        scatter_dimension=0,
        tiled=True,
    )
    back_dx = send_back(expert_dx[None])[0]
    out_slots = back_out.reshape(slot_total, model_width)
    dx_slots = back_dx.reshape(slot_total, model_width)
    per_choice = jnp.dot(selector.T, out_slots, preferred_element_type=jnp.float32)
    per_choice = per_choice.reshape(tok_rows, top_count, model_width)
    mixed = jnp.sum(router_probs[:, :, None] * per_choice, axis=1).astype(jnp.bfloat16)
    prob_grad = jnp.sum(out_grad.astype(jnp.float32)[:, None, :] * per_choice, axis=2)
    input_grad = jnp.dot(by_token.T, dx_slots, preferred_element_type=jnp.float32).astype(
        jnp.bfloat16
    )
    return (mixed, input_grad, prob_grad, grad_gate, grad_up, grad_down)


def solution(mesh):
    in_specs = (
        P(("dp", "expert"), None),
        P(("dp", "expert"), None),
        P(("dp", "expert"), None),
        P("expert", "dp", None),
        P("expert", "dp", None),
        P("expert", "dp", None),
        P(("dp", "expert"), None),
    )
    out_specs = (
        P(("dp", "expert"), None),
        P(("dp", "expert"), None),
        P(("dp", "expert"), None),
        P("expert", "dp", None),
        P("expert", "dp", None),
        P("expert", "dp", None),
    )
    return jax.shard_map(
        on_device, mesh=mesh, in_specs=in_specs, out_specs=out_specs, check_vma=False
    )
```

profile of v0, /device:TPU:0, one launch (start us, length us, event | category | flops | bytes accessed | tf_op | source)
XLA Modules:
  0.0 847.3 jit_solution(7481087154159858697)
XLA Ops:
  17.9 37.4 %all_to_all.20 = bf16[1,8,1,36,4096]{4,3,2,0,1:T(8,128)(2,1)S(1)} all-to-all(bf16[1,8,1,36,4096]{4,3,2,0,1:T(8,128)(2,1)} %bitcast.136), channel_id=1, replica_groups=mesh['dp'=4,'expert'=8] {'expert'}, dimensions={1} | all-to-all | bytes 4718592 | tf_op jit(solution)/shard_map/all_to_all | solution.py:8
  63.2 6.5 convert_element_type.98
  69.7 4.8 convolution_convert_fusion
  78.6 35.7 %all_to_all.21 = bf16[1,8,1,36,4096]{4,3,2,0,1:T(8,128)(2,1)S(1)} all-to-all(bf16[1,8,1,36,4096]{4,3,2,0,1:T(8,128)(2,1)} %bitcast.137), channel_id=1, replica_groups=mesh['dp'=4,'expert'=8] {'expert'}, dimensions={1} | all-to-all | bytes 4718592 | tf_op jit(solution)/shard_map/all_to_all | solution.py:8
  117.4 106.8 %all-gather.5.cloned.1.call-done = bf16[4,8,1,36,4096]{4,1,3,2,0:T(8,128)(2,1)} async-done(((bf16[1,8,1,36,4096]{4,1,3,2,0:T(8,128)(2,1)}), bf16[4,8,1,36,4096]{4,1,3,2,0:T(8,128)(2,1)}) %all-gather.5.cloned.1.call-update) | async-done | bytes 9437200 | tf_op jit(solution)/shard_map/all_gather | solution.py:9
  224.2 13.6 %copy.57 = bf16[4,8,1,36,4096]{4,3,1,0,2:T(8,128)(2,1)} copy(bf16[4,8,1,36,4096]{4,1,3,2,0:T(8,128)(2,1)} %all-gather.5.cloned.1.call-done) | data formatting | bytes 18874368 | tf_op jit(solution)/shard_map/all_gather | solution.py:9
  237.8 8.8 %fusion.21 = f32[32,1,36,256]{3,2,0,1:T(8,128)} fusion(bf16[32,36,4096]{2,1,0:T(8,128)(2,1)} %bitcast.128, bf16[1,256,4096]{2,1,0:T(8,128)(2,1)} %param.11), kind=kOutput, calls=%fused_computation.30 | convolution fusion | flops 2415919104 | bytes 12713984 | tf_op jit(solution)/shard_map/sxmd,xfd->sxmf/dot_general | solution.py:47
  246.7 4.3 fusion.18
  251.0 139.8 %all-gather.7.cloned.1.call-done = bf16[4,8,1,36,4096]{4,1,3,2,0:T(8,128)(2,1)} async-done(((bf16[1,8,1,36,4096]{4,1,3,2,0:T(8,128)(2,1)}), bf16[4,8,1,36,4096]{4,1,3,2,0:T(8,128)(2,1)}) %all-gather.7.cloned.1.call-update) | async-done | bytes 9437200 | tf_op jit(solution)/shard_map/all_gather | solution.py:9
  390.8 13.5 %copy.64 = bf16[4,8,1,36,4096]{4,3,1,0,2:T(8,128)(2,1)} copy(bf16[4,8,1,36,4096]{4,1,3,2,0:T(8,128)(2,1)} %all-gather.7.cloned.1.call-done) | data formatting | bytes 18874368 | tf_op jit(solution)/shard_map/all_gather | solution.py:9
  404.2 9.2 %fusion.29 = (bf16[32,36,256]{2,1,0:T(8,128)(2,1)}, bf16[32,1,36,256]{3,2,0,1:T(8,128)(2,1)S(1)}, bf16[32,36,256]{2,1,0:T(8,128)(2,1)S(1)}) fusion(f32[32,1,36,256]{3,2,0,1:T(8,128)} %fusion.18, f32[32,1,36,256]{3,2,0,1:T(8,128)} %fusion.21, bf16[32,36,4096]{2,1,0:T(8,128)(2,1)} %bitcast.134, bf16[1,256,4096]{2,1,0:T(8,128)(2,1)S(1)} %copy-done), kind=kOutput, calls=%fused_computation.38 | convolution fusion | flops 2420342784 | bytes 15663104 | tf_op jit(solution)/shard_map/sxmd,xfd->sxmf/dot_general | solution.py:61
  413.4 8.7 %fusion.13 = f32[32,36,4096]{2,1,0:T(8,128)} fusion(bf16[1,256,4096]{2,1,0:T(8,128)(2,1)S(1)} %copy-done.5, bf16[32,1,36,256]{3,2,0,1:T(8,128)(2,1)S(1)} %get-tuple-element.9), kind=kOutput, calls=%fused_computation.24 | convolution fusion | flops 2415919104 | bytes 21561344 | tf_op jit(solution)/shard_map/sxmf,xfd->sxmd/dot_general | solution.py:75
  422.1 14.6 %fusion = bf16[32,1,36,4096]{3,2,0,1:T(8,128)(2,1)} fusion(f32[32,36,4096]{2,1,0:T(8,128)} %fusion.13, bf16[32,36,256]{2,1,0:T(8,128)(2,1)} %get-tuple-element.8, bf16[1,256,4096]{2,1,0:T(8,128)(2,1)} %param.11), kind=kOutput, calls=%fused_computation.1 | convolution fusion | flops 2425356288 | bytes 30998528 | tf_op jit(solution)/shard_map/sxmf,xfd->sxmd/dot_general | solution.py:78
  436.8 5.9 convert_bitcast_fusion
  442.7 170.4 %reduce-scatter.5.cloned.1.call-done = bf16[8,1,36,4096]{3,2,0,1:T(8,128)(2,1)} async-done(((bf16[32,1,36,4096]{3,2,0,1:T(8,128)(2,1)}), bf16[8,1,36,4096]{3,2,0,1:T(8,128)(2,1)}) %reduce-scatter.5.cloned.1.call-update) | async-done | bytes 2359312 | tf_op jit(solution)/shard_map/reduce_scatter | solution.py:76
  613.2 4.4 all-to-all-start.3
  622.8 171.7 %reduce-scatter.3.cloned.1.call-done = bf16[8,1,36,4096]{3,2,0,1:T(8,128)(2,1)} async-done(((bf16[32,1,36,4096]{3,2,0,1:T(8,128)(2,1)}), bf16[8,1,36,4096]{3,2,0,1:T(8,128)(2,1)}) %reduce-scatter.3.cloned.1.call-update) | async-done | bytes 2359312 | tf_op jit(solution)/shard_map/reduce_scatter | solution.py:51
  794.5 4.6 all-to-all-start.1
  799.2 8.3 fusion.4
  807.4 8.3 fusion.5
  815.7 4.1 fusion.6
  819.8 4.1 reshape_squeeze.9
  831.4 4.1 reshape.153
  835.5 5.1 multiply_reduce_fusion
  (59 shorter events, 38.5 us)
Async XLA Ops:
  7.2 397.1 %copy-start = (bf16[1,256,4096]{2,1,0:T(8,128)(2,1)S(1)}, bf16[1,256,4096]{2,1,0:T(8,128)(2,1)}, u32[]{:S(2)}) copy-start(bf16[1,256,4096]{2,1,0:T(8,128)(2,1)} %param.12) | copy-start | bytes 6291460
  7.2 217.0 %all-gather.5.cloned.1.call-start = ((), (), s32[]{:S(2)}) async-start(), calls=%async_computation.8 | async-start | bytes 11796480 | tf_op jit(solution)/shard_map/all_gather | solution.py:9
  57.9 0.7 copy-start.7
  57.9 1.2 copy-start.2
  57.9 332.8 %all-gather.7.cloned.1.call-start = ((), (), s32[]{:S(2)}) async-start(), calls=%async_computation.9 | async-start | bytes 11796480 | tf_op jit(solution)/shard_map/all_gather | solution.py:9
  117.1 496.1 %reduce-scatter.5.cloned.1.call-start = ((), (), s32[]{:S(2)}) async-start(), calls=%async_computation.7 | async-start | bytes 13107200 | tf_op jit(solution)/shard_map/reduce_scatter | solution.py:76
  237.8 8.9 %copy-start.1 = (bf16[4,8,1,36,4096]{4,3,1,0,2:T(8,128)(2,1)S(1)}, bf16[4,8,1,36,4096]{4,3,1,0,2:T(8,128)(2,1)}, u32[]{:S(2)}) copy-start(bf16[4,8,1,36,4096]{4,3,1,0,2:T(8,128)(2,1)} %copy.57) | copy-start | bytes 28311556
  237.8 8.9 %copy-start.4 = (bf16[1,256,4096]{2,1,0:T(8,128)(2,1)S(1)}, bf16[1,256,4096]{2,1,0:T(8,128)(2,1)}, u32[]{:S(2)}) copy-start(bf16[1,256,4096]{2,1,0:T(8,128)(2,1)} %param.10) | copy-start | bytes 6291460
  404.2 9.2 %copy-start.5 = (bf16[1,256,4096]{2,1,0:T(8,128)(2,1)S(1)}, bf16[1,256,4096]{2,1,0:T(8,128)(2,1)}, u32[]{:S(2)}) copy-start(bf16[1,256,4096]{2,1,0:T(8,128)(2,1)} %param.10) | copy-start | bytes 6291460
  436.8 357.7 %reduce-scatter.3.cloned.1.call-start = ((), (), s32[]{:S(2)}) async-start(), calls=%async_computation.6 | async-start | bytes 13107200 | tf_op jit(solution)/shard_map/reduce_scatter | solution.py:51
  613.2 181.3 %all-to-all-start.3 = ((bf16[1,8,1,36,4096]{4,3,2,0,1:T(8,128)(2,1)}), bf16[1,8,1,36,4096]{4,3,2,0,1:T(8,128)(2,1)}, u32[]{:S(2)}, u32[]{:S(2)}) async-start(bf16[1,8,1,36,4096]{4,3,2,0,1:T(8,128)(2,1)} %bitcast.139), calls=%async_computation.5 | async-start | bytes 5242880 | tf_op jit(solution)/shard_map/all_to_all | solution.py:14
  794.5 36.9 %all-to-all-start.1 = ((bf16[1,8,1,36,4096]{4,3,2,0,1:T(8,128)(2,1)}), bf16[1,8,1,36,4096]{4,3,2,0,1:T(8,128)(2,1)}, u32[]{:S(2)}, u32[]{:S(2)}) async-start(bf16[1,8,1,36,4096]{4,3,2,0,1:T(8,128)(2,1)} %bitcast.138), calls=%async_computation.2 | async-start | bytes 5242880 | tf_op jit(solution)/shard_map/all_to_all | solution.py:14
  799.1 8.3 copy-start.3
  799.1 16.5 %slice-start = ((s8[10485760]{0:T(1024)(128)(4,1)}), s8[4194304]{0:T(1024)(128)(4,1)S(1)}, s32[]{:S(2)}) async-start(s8[10485760]{0:T(1024)(128)(4,1)} %bitcast.131), calls=%async_computation.10 | async-start | bytes 8388608
  799.2 16.5 %slice-start.1 = ((s8[10485760]{0:T(1024)(128)(4,1)}), s8[4194304]{0:T(1024)(128)(4,1)S(1)}, s32[]{:S(2)}) async-start(s8[10485760]{0:T(1024)(128)(4,1)} %bitcast.131), calls=%async_computation.11 | async-start | bytes 8388608
  807.4 8.3 slice-start.2
  827.3 8.2 copy-start.6
Sparse Core Ops, SparseCore 0:
  58.1 166.1 all-gather.4
  225.8 164.9 all-gather.6
  436.9 176.2 reduce-scatter.4
  615.4 179.0 reduce-scatter.2
where the time goes:
time: 854 us; the launch traced here: 847 us
  waiting for transfers between devices  593 us (69%)
  matrix products  88.9 us (10%)
  blocking collectives  73.1 us (9%)
  local copies, waits for them, and re-layouts  63.9 us (7%)
  between operations  14.1 us (2%)
  starting transfers between devices  9.51 us (1%)
    all_gather x2, waiting for transfers between devices, deliver(): arrived = lax.all_gather(moved_rows[None], 'dp', axis=0, tiled=True)  247 us
    reduce_scatter x1, waiting for transfers between devices, on_device(): lax.psum_scatter(jnp.einsum('sxmf,xfd->sxmd', hidden, w_down, preferred_e...  172 us
    reduce_scatter x1, waiting for transfers between devices, on_device(): lax.psum_scatter((total + jnp.einsum('sxmf,xfd->sxmd', d_up, w_up, prefer...  170 us
    all_to_all x2, blocking collectives, deliver(): lax.all_to_all(stacked, 'expert', split_axis=1, concat_axis=1, tiled=True)  73.1 us
    all_gather x2, local copies, waits for them, and re-layouts, deliver(): arrived = lax.all_gather(moved_rows[None], 'dp', axis=0, tiled=True)  27 us
  transfers between devices with their start and end apart: 6, of which 5 were waited for; matrix products, arithmetic and copies ran while one was open for 10% of the time, Pallas kernels for 0%

commit v1 on v0

--- a/solution.py
+++ b/solution.py
@@ -6,7 +6,9 @@
 
 def deliver(stacked):
     moved_rows = lax.all_to_all(stacked, "expert", split_axis=1, concat_axis=1, tiled=True)
-    arrived = lax.all_gather(moved_rows[None], "dp", axis=0, tiled=True)
+    arrived = jnp.concatenate(
+        lax.all_to_all(jnp.stack([moved_rows[None]] * lax.axis_size("dp")), "dp", 0, 0), axis=0
+    )
     return arrived
 
 

time: 854 us -> 993 us (1.16)
  waiting for transfers between devices: 593 us -> 768 us
  blocking collectives: 73.1 us -> 0 us
  starting transfers between devices: 9.51 us -> 31 us
  local copies, waits for them, and re-layouts: 63.9 us -> 78.3 us
    all_to_all x0 -> x4, waiting for transfers between devices: none -> 418 us  [the longest x2 377 us: deliver(): lax.all_to_all(jnp.stack([moved_rows[None]] * lax.axis_size('dp')), 'dp',...]
    all_gather x2 -> x0, waiting for transfers between devices: 247 us -> none  [deliver(): arrived = lax.all_gather(moved_rows[None], 'dp', axis=0, tiled=True)]
    all_to_all x2 -> x0, blocking collectives: 73.1 us -> none  [deliver(): lax.all_to_all(stacked, 'expert', split_axis=1, concat_axis=1, tiled=True)]
    all_gather x2 -> x0, local copies, waits for them, and re-layouts: 27 us -> none  [deliver(): arrived = lax.all_gather(moved_rows[None], 'dp', axis=0, tiled=True)]
    all_to_all x0 -> x2, local copies, waits for them, and re-layouts: none -> 26.2 us  [deliver(): lax.all_to_all(jnp.stack([moved_rows[None]] * lax.axis_size('dp')), 'dp',...]
    all_to_all x0 -> x4, starting transfers between devices: none -> 21.3 us  [the longest x2 11.6 us: deliver(): lax.all_to_all(jnp.stack([moved_rows[None]] * lax.axis_size('dp')), 'dp',...]
    another operation x1 -> x3, local copies, waits for them, and re-layouts: 0.01 us -> 12.9 us  [the longest x2 12.9 us: deliver(): jnp.stack([moved_rows[None]] * lax.axis_size('dp'))]
  transfers between devices with their start and end apart: 6 -> 8, of which waited for: 5 -> 7; matrix products, arithmetic and copies ran while one was open for 10% -> 9% of each run, Pallas kernels for 0% -> 0%
where the time goes in v1:
time: 993 us; the launch traced here: 985 us
  waiting for transfers between devices  768 us (77%)
  matrix products  88.1 us (9%)
  local copies, waits for them, and re-layouts  78.3 us (8%)
  starting transfers between devices  31 us (3%)
  between operations  14.5 us (1%)
    all_to_all x2, waiting for transfers between devices, deliver(): lax.all_to_all(jnp.stack([moved_rows[None]] * lax.axis_size('dp')), 'dp',...  377 us
    reduce_scatter x1, waiting for transfers between devices, on_device(): lax.psum_scatter((total + jnp.einsum('sxmf,xfd->sxmd', d_up, w_up, prefer...  173 us
    reduce_scatter x1, waiting for transfers between devices, on_device(): lax.psum_scatter(jnp.einsum('sxmf,xfd->sxmd', hidden, w_down, preferred_e...  172 us
    all_to_all x2, waiting for transfers between devices, deliver(): lax.all_to_all(stacked, 'expert', split_axis=1, concat_axis=1, tiled=True)  41.1 us
    all_to_all x2, local copies, waits for them, and re-layouts, deliver(): lax.all_to_all(jnp.stack([moved_rows[None]] * lax.axis_size('dp')), 'dp',...  26.2 us
  transfers between devices with their start and end apart: 8, of which 7 were waited for; matrix products, arithmetic and copies ran while one was open for 9% of the time, Pallas kernels for 0%

profile of v1, /device:TPU:0, one launch (start us, length us, event | category | flops | bytes accessed | tf_op | source)
XLA Modules:
  0.0 984.6 jit_solution(52300269903384151)
XLA Ops:
  17.8 5.3 all-to-all-start
  27.5 6.1 convert_element_type.98
  42.2 13.3 %all-to-all-done = bf16[1,8,1,36,4096]{4,3,2,0,1:T(8,128)(2,1)} async-done(((bf16[1,8,1,36,4096]{4,3,2,0,1:T(8,128)(2,1)}), bf16[1,8,1,36,4096]{4,3,2,0,1:T(8,128)(2,1)}, u32[]{:S(2)}, u32[]{:S(2)}) %all-to-all-start) | async-done | bytes 2359328 | tf_op jit(solution)/shard_map/all_to_all | solution.py:8
  64.4 27.8 %all-to-all-done.3 = bf16[1,8,1,36,4096]{4,3,2,0,1:T(8,128)(2,1)} async-done(((bf16[1,8,1,36,4096]{4,3,2,0,1:T(8,128)(2,1)}), bf16[1,8,1,36,4096]{4,3,2,0,1:T(8,128)(2,1)}, u32[]{:S(2)}, u32[]{:S(2)}) %all-to-all-start.3) | async-done | bytes 2359328 | tf_op jit(solution)/shard_map/all_to_all | solution.py:8
  92.2 6.5 stack.6
  98.7 5.8 all-to-all-start.1
  104.5 4.5 copy.63
  109.0 199.0 %all-to-all-done.1 = bf16[4,1,1,8,1,36,4096]{6,3,5,4,2,1,0:T(8,128)(2,1)} async-done(((bf16[4,1,1,8,1,36,4096]{6,3,5,4,2,1,0:T(8,128)(2,1)}), bf16[4,1,1,8,1,36,4096]{6,3,5,4,2,1,0:T(8,128)(2,1)}, u32[]{:S(2)}, u32[]{:S(2)}) %all-to-all-start.1) | async-done | bytes 9437216 | tf_op jit(solution)/shard_map/all_to_all | solution.py:10
  308.0 6.4 stack.7
  314.4 5.8 all-to-all-start.4
  320.8 13.1 %copy.57 = bf16[4,1,1,8,1,36,4096]{6,5,3,0,4,2,1:T(8,128)(2,1)} copy(bf16[4,1,1,8,1,36,4096]{6,3,5,4,2,1,0:T(8,128)(2,1)} %all-to-all-done.1) | data formatting | bytes 18874368 | tf_op jit(solution)/shard_map/all_to_all | solution.py:10
  333.8 8.8 fusion.21
  347.0 178.2 %all-to-all-done.4 = bf16[4,1,1,8,1,36,4096]{6,3,5,4,2,1,0:T(8,128)(2,1)} async-done(((bf16[4,1,1,8,1,36,4096]{6,3,5,4,2,1,0:T(8,128)(2,1)}), bf16[4,1,1,8,1,36,4096]{6,3,5,4,2,1,0:T(8,128)(2,1)}, u32[]{:S(2)}, u32[]{:S(2)}) %all-to-all-start.4) | async-done | bytes 9437216 | tf_op jit(solution)/shard_map/all_to_all | solution.py:10
  525.2 13.1 %copy.64 = bf16[4,1,1,8,1,36,4096]{6,5,3,0,4,2,1:T(8,128)(2,1)} copy(bf16[4,1,1,8,1,36,4096]{6,3,5,4,2,1,0:T(8,128)(2,1)} %all-to-all-done.4) | data formatting | bytes 18874368 | tf_op jit(solution)/shard_map/all_to_all | solution.py:10
  538.3 9.2 fusion.29
  547.5 8.8 fusion.13
  556.2 14.6 %fusion = bf16[32,1,36,4096]{3,2,0,1:T(8,128)(2,1)} fusion(f32[32,36,4096]{2,1,0:T(8,128)} %fusion.13, bf16[32,36,256]{2,1,0:T(8,128)(2,1)} %get-tuple-element.8, bf16[1,256,4096]{2,1,0:T(8,128)(2,1)} %param.11), kind=kOutput, calls=%fused_computation.1 | convolution fusion | flops 2425356288 | bytes 30998528 | tf_op jit(solution)/shard_map/sxmf,xfd->sxmd/dot_general | solution.py:80
  570.9 5.5 convert_bitcast_fusion
  576.5 173.4 %reduce-scatter.5.cloned.1.call-done = bf16[8,1,36,4096]{3,2,0,1:T(8,128)(2,1)} async-done(((bf16[32,1,36,4096]{3,2,0,1:T(8,128)(2,1)}), bf16[8,1,36,4096]{3,2,0,1:T(8,128)(2,1)}) %reduce-scatter.5.cloned.1.call-update) | async-done | bytes 2359312 | tf_op jit(solution)/shard_map/reduce_scatter | solution.py:78
  759.5 171.8 %reduce-scatter.3.cloned.1.call-done = bf16[8,1,36,4096]{3,2,0,1:T(8,128)(2,1)} async-done(((bf16[32,1,36,4096]{3,2,0,1:T(8,128)(2,1)}), bf16[8,1,36,4096]{3,2,0,1:T(8,128)(2,1)}) %reduce-scatter.3.cloned.1.call-update) | async-done | bytes 2359312 | tf_op jit(solution)/shard_map/reduce_scatter | solution.py:53
  931.4 4.7 all-to-all-start.2
  936.1 8.3 fusion.4
  944.4 8.3 fusion.5
  972.4 5.1 multiply_reduce_fusion
  (61 shorter events, 66.8 us)
Async XLA Ops:
  7.2 531.1 %copy-start = (bf16[1,256,4096]{2,1,0:T(8,128)(2,1)S(1)}, bf16[1,256,4096]{2,1,0:T(8,128)(2,1)}, u32[]{:S(2)}) copy-start(bf16[1,256,4096]{2,1,0:T(8,128)(2,1)} %param.12) | copy-start | bytes 6291460
  17.8 5.3 copy-start.7
  17.8 5.6 copy-start.2
  17.8 37.7 %all-to-all-start = ((bf16[1,8,1,36,4096]{4,3,2,0,1:T(8,128)(2,1)}), bf16[1,8,1,36,4096]{4,3,2,0,1:T(8,128)(2,1)}, u32[]{:S(2)}, u32[]{:S(2)}) async-start(bf16[1,8,1,36,4096]{4,3,2,0,1:T(8,128)(2,1)} %bitcast.138), calls=%async_computation | async-start | bytes 5242880 | tf_op jit(solution)/shard_map/all_to_all | solution.py:8
  55.5 36.6 %all-to-all-start.3 = ((bf16[1,8,1,36,4096]{4,3,2,0,1:T(8,128)(2,1)}), bf16[1,8,1,36,4096]{4,3,2,0,1:T(8,128)(2,1)}, u32[]{:S(2)}, u32[]{:S(2)}) async-start(bf16[1,8,1,36,4096]{4,3,2,0,1:T(8,128)(2,1)} %bitcast.139), calls=%async_computation.4 | async-start | bytes 5242880 | tf_op jit(solution)/shard_map/all_to_all | solution.py:8
  98.7 209.3 %all-to-all-start.1 = ((bf16[4,1,1,8,1,36,4096]{6,3,5,4,2,1,0:T(8,128)(2,1)}), bf16[4,1,1,8,1,36,4096]{6,3,5,4,2,1,0:T(8,128)(2,1)}, u32[]{:S(2)}, u32[]{:S(2)}) async-start(bf16[4,1,1,8,1,36,4096]{6,3,5,4,2,1,0:T(8,128)(2,1)} %stack.6), calls=%async_computation.1 | async-start | bytes 18874368 | tf_op jit(solution)/shard_map/all_to_all | solution.py:10
  314.4 210.8 %all-to-all-start.4 = ((bf16[4,1,1,8,1,36,4096]{6,3,5,4,2,1,0:T(8,128)(2,1)}), bf16[4,1,1,8,1,36,4096]{6,3,5,4,2,1,0:T(8,128)(2,1)}, u32[]{:S(2)}, u32[]{:S(2)}) async-start(bf16[4,1,1,8,1,36,4096]{6,3,5,4,2,1,0:T(8,128)(2,1)} %stack.7), calls=%async_computation.5 | async-start | bytes 18874368 | tf_op jit(solution)/shard_map/all_to_all | solution.py:10
  320.2 429.7 %reduce-scatter.5.cloned.1.call-start = ((), (), s32[]{:S(2)}) async-start(), calls=%async_computation.9 | async-start | bytes 13107200 | tf_op jit(solution)/shard_map/reduce_scatter | solution.py:78
  333.8 8.8 copy-start.1
  333.8 8.8 copy-start.4
  538.3 9.2 copy-start.5
  570.9 360.5 %reduce-scatter.3.cloned.1.call-start = ((), (), s32[]{:S(2)}) async-start(), calls=%async_computation.8 | async-start | bytes 13107200 | tf_op jit(solution)/shard_map/reduce_scatter | solution.py:53
  749.9 181.5 %all-to-all-start.5 = ((bf16[1,8,1,36,4096]{4,3,2,0,1:T(8,128)(2,1)}), bf16[1,8,1,36,4096]{4,3,2,0,1:T(8,128)(2,1)}, u32[]{:S(2)}, u32[]{:S(2)}) async-start(bf16[1,8,1,36,4096]{4,3,2,0,1:T(8,128)(2,1)} %bitcast.141), calls=%async_computation.7 | async-start | bytes 5242880 | tf_op jit(solution)/shard_map/all_to_all | solution.py:16
  931.4 36.9 %all-to-all-start.2 = ((bf16[1,8,1,36,4096]{4,3,2,0,1:T(8,128)(2,1)}), bf16[1,8,1,36,4096]{4,3,2,0,1:T(8,128)(2,1)}, u32[]{:S(2)}, u32[]{:S(2)}) async-start(bf16[1,8,1,36,4096]{4,3,2,0,1:T(8,128)(2,1)} %bitcast.140), calls=%async_computation.3 | async-start | bytes 5242880 | tf_op jit(solution)/shard_map/all_to_all | solution.py:16
  936.1 8.3 copy-start.3
  936.1 16.5 %slice-start = ((s8[10485760]{0:T(1024)(128)(4,1)}), s8[4194304]{0:T(1024)(128)(4,1)S(1)}, s32[]{:S(2)}) async-start(s8[10485760]{0:T(1024)(128)(4,1)} %bitcast.133), calls=%async_computation.10 | async-start | bytes 8388608
  936.1 16.5 %slice-start.1 = ((s8[10485760]{0:T(1024)(128)(4,1)}), s8[4194304]{0:T(1024)(128)(4,1)S(1)}, s32[]{:S(2)}) async-start(s8[10485760]{0:T(1024)(128)(4,1)} %bitcast.133), calls=%async_computation.11 | async-start | bytes 8388608
  944.4 8.3 slice-start.2
  964.2 8.2 copy-start.6
Sparse Core Ops, SparseCore 0:
  571.0 178.8 reduce-scatter.4
  752.3 179.0 reduce-scatter.2
